TPU v7x, 32 devices: a whole 2x2x4 slice. The times are simulated.
32 devices in a mesh: row: 4 (over z), col: 8 (over y, x, core).
Axes of the slice: x: 2, y: 2, z: 4, core: 2. Of those that a mesh axis runs over, the one named last changes fastest.
Arguments:
- table: float32 [32, 512, 512], P(None, 'row', 'col'), may hold values from -50 to 50
- in_weight: bfloat16 [2, 128, 128], replicated, may hold values from -0.5 to 0.5
- in_bias: float32 [2, 128], replicated, may hold values from -3 to 3
- mid_weight: bfloat16 [2, 128, 128], replicated, may hold values from -0.5 to 0.5
- mid_bias: float32 [2, 128], replicated, may hold values from -3 to 3
- out_weight: bfloat16 [2, 128, 32], replicated, may hold values from -0.5 to 0.5
- out_bias: float32 [2, 32], replicated, may hold values from -3 to 3
Outputs:
- out_table: float32 [32, 512, 512], P(None, 'row', 'col')
All inputs are finite; a program needn't handle non-finite values.
Results may differ from a plain program's by a relative error of at most 0.0068.
Values may be sent and summed in bfloat16 or wider, within the bound.
A program may use at most 64 MiB of HBM per device.

v0:
```python
import math

import jax
import jax.numpy as jnp
from jax import lax
from jax.sharding import PartitionSpec as P


def to_strips(tile_in):
    return lax.all_to_all(tile_in, "col", split_axis=1, concat_axis=2, tiled=True)


def swap_strips(strips):
    channels, piece_rows, entities = strips.shape
    devices = lax.axis_size("row") * lax.axis_size("col")
    sectioned = strips.reshape(channels, piece_rows, devices, piece_rows).transpose(0, 2, 3, 1)
    sectioned = sectioned.reshape(channels, devices, piece_rows * piece_rows)
    swapped = lax.all_to_all(sectioned, ("row", "col"), split_axis=1, concat_axis=1, tiled=True)
    regrouped = swapped.reshape(channels, devices, piece_rows, piece_rows).transpose(0, 2, 1, 3)
    return regrouped.reshape(channels, piece_rows, entities)


def reverse_tile(tile_in):
    regrouped = swap_strips(to_strips(tile_in))
    return lax.all_to_all(regrouped, "col", split_axis=2, concat_axis=1, tiled=True)


def pooled(values, pool_scale):
    row_pool = lax.psum(jnp.sum(values, axis=2), "col") * pool_scale
    col_pool = lax.psum(jnp.sum(values, axis=1), "row") * pool_scale
    return (row_pool, col_pool)


def evaluate(
    own_part,
    pair_part,
    row_pool,
    col_pool,
    in_weight,
    in_bias,
    mid_weight,
    mid_bias,
    out_weight,
    out_bias,
    layer_idx,
    mirrored,
):
    channels = own_part.shape[0]
    w_first = in_weight[layer_idx]
    w_own = w_first[:channels]
    w_pair = w_first[channels : 2 * channels]
    w_row = w_first[2 * channels : 3 * channels]
    w_col = w_first[3 * channels :]
    if mirrored:
        w_row, w_col = (w_col, w_row)
    mid_mat = mid_weight[layer_idx]
    out_mat = out_weight[layer_idx]
    mid_shift = mid_bias[layer_idx]
    out_shift = out_bias[layer_idx]
    row_term = jnp.einsum(
        "ck,cr->kr", w_row, row_pool.astype(jnp.bfloat16), preferred_element_type=jnp.float32
    )
    col_term = jnp.einsum(
        "ck,cj->kj", w_col, col_pool.astype(jnp.bfloat16), preferred_element_type=jnp.float32
    )
    col_term = col_term + in_bias[layer_idx][:, None]
    row_count = own_part.shape[1]
    col_count = own_part.shape[2]
    split_count = math.gcd(4, row_count)
    block_rows = row_count // split_count
    result = jnp.zeros((out_mat.shape[1], row_count, col_count), jnp.float32)

    def fill_block(block_idx, result):
        row_start = block_idx * block_rows
        own_rows = lax.dynamic_slice_in_dim(own_part, row_start, block_rows, 1).astype(jnp.bfloat16)
        pair_rows = lax.dynamic_slice_in_dim(pair_part, row_start, block_rows, 1).astype(
            jnp.bfloat16
        )
        row_share = lax.dynamic_slice_in_dim(row_term, row_start, block_rows, 1)
        first_pre = jnp.einsum("ck,crj->krj", w_own, own_rows, preferred_element_type=jnp.float32)
        first_pre = first_pre + jnp.einsum(
            "ck,crj->krj", w_pair, pair_rows, preferred_element_type=jnp.float32
        )
        first_pre = first_pre + row_share[:, :, None] + col_term[:, None, :]
        hidden = jax.nn.relu(first_pre).astype(jnp.bfloat16)
        second = (
            jnp.einsum("hk,hrj->krj", mid_mat, hidden, preferred_element_type=jnp.float32)
            + mid_shift[:, None, None]
        )
        second = jax.nn.relu(second).astype(jnp.bfloat16)
        final_out = (
            jnp.einsum("kc,krj->crj", out_mat, second, preferred_element_type=jnp.float32)
            + out_shift[:, None, None]
        )
        return lax.dynamic_update_slice_in_dim(result, final_out, row_start, 1)

    return lax.fori_loop(0, split_count, fill_block, result)


def body(table, in_weight, in_bias, mid_weight, mid_bias, out_weight, out_bias):
    tile_rows = table.shape[1]
    tile_cols = table.shape[2]
    entities = tile_rows * lax.axis_size("row")
    pool_scale = 1.0 / math.sqrt(entities)
    weights = (in_weight, in_bias, mid_weight, mid_bias, out_weight, out_bias)
    row_pool, col_pool = pooled(table, pool_scale)
    every_col = lax.all_gather(col_pool, "col", axis=1, tiled=True)
    every_row = lax.all_gather(row_pool.astype(jnp.bfloat16), "row", axis=1, tiled=True).astype(
        row_pool.dtype
    )
    reversed_one = reverse_tile(table.astype(jnp.bfloat16))
    first_out = evaluate(table, reversed_one, row_pool, col_pool, *weights, 0, False)
    pool_at_rows = lax.dynamic_slice_in_dim(
        every_col, lax.axis_index("row") * tile_rows, tile_rows, 1
    )
    pool_at_cols = lax.dynamic_slice_in_dim(
        every_row, lax.axis_index("col") * tile_cols, tile_cols, 1
    )
    mirror_out = evaluate(reversed_one, table, pool_at_rows, pool_at_cols, *weights, 0, True)
    reversed_two = mirror_out.astype(jnp.bfloat16)
    row_again, col_again = pooled(first_out, pool_scale)
    return evaluate(first_out, reversed_two, row_again, col_again, *weights, 1, False)


def solution(mesh):
    placed = (P(None, "row", "col"), P(), P(), P(), P(), P(), P())
    return jax.shard_map(
        body, mesh=mesh, in_specs=placed, out_specs=P(None, "row", "col"), check_vma=False
    )
```

profile of v0, /device:TPU:0, one launch (start us, length us, event | category | flops | bytes accessed | tf_op | source)
XLA Modules:
  0.0 215.7 jit_solution(13248701874130544638)
XLA Ops:
  0.0 2.2 %fusion.99 = (f32[32,64]{1,0:T(8,128)S(1)}, f32[32,128]{1,0:T(8,128)S(1)}, bf16[32,128,64]{1,2,0:T(8,128)(2,1)S(1)}) fusion(f32[32,128,64]{1,2,0:T(8,128)} %param.13), kind=kLoop, calls=%fused_computation.129 | loop fusion | flops 780288 | bytes 1597440 | tf_op jit(solution)/shard_map/reduce_sum | solution.py:30
  2.3 1.6 copy.87
  3.9 1.5 reshape.53
  5.4 5.2 %all-to-all-start = ((bf16[8,2,16384]{2,1,0:T(2,128)(2,1)}), bf16[8,2,16384]{2,1,0:T(2,128)(2,1)S(1)}, u32[]{:S(2)}, u32[]{:S(2)}) async-start(bf16[8,2,16384]{2,1,0:T(2,128)(2,1)} %reshape.53), calls=%async_computation | async-start | bytes 1048576 | tf_op jit(solution)/shard_map/all_to_all | solution.py:10
  10.6 26.6 %psum.28 = f32[32,128]{1,0:T(8,128)S(1)} all-reduce(f32[32,128]{1,0:T(8,128)S(1)} %get-tuple-element.776), channel_id=1, replica_groups=mesh['row'=4,'col'=8] {'col'}, use_global_device_ids=true, to_apply=%region_1.0 | all-reduce | flops 4096 | bytes 32768 | tf_op jit(solution)/shard_map/psum | solution.py:29
  37.2 19.0 %psum.29 = f32[32,64]{1,0:T(8,128)S(1)} all-reduce(f32[32,64]{1,0:T(8,128)S(1)} %get-tuple-element.775), channel_id=1, replica_groups=mesh['row'=4,'col'=8] {'row'}, use_global_device_ids=true, to_apply=%region_3.0 | all-reduce | flops 2048 | bytes 16384 | tf_op jit(solution)/shard_map/psum | solution.py:30
  56.9 1.9 copy.89
  58.8 5.1 %copy.90 = bf16[32,32,16,16]{1,3,2,0:T(8,128)(2,1)S(1)} copy(bf16[32,32,16,16]{0,2,1,3:T(8,128)(2,1)} %bitcast.248) | data formatting | bytes 1048576 | tf_op jit(solution)/shard_map/transpose | solution.py:16
  64.0 1.8 copy.91
  65.7 2.6 %all-to-all-start.1 = ((bf16[32,32,256]{2,0,1:T(8,128)(2,1)}), bf16[32,32,256]{2,0,1:T(8,128)(2,1)S(1)}, u32[]{:S(2)}, u32[]{:S(2)}) async-start(bf16[32,32,256]{2,0,1:T(8,128)(2,1)} %copy.91), calls=%async_computation.1 | async-start | bytes 1048576 | tf_op jit(solution)/shard_map/all_to_all | solution.py:18
  68.4 9.6 %all-gather = bf16[8,64,32]{1,2,0:T(8,128)(2,1)S(1)} all-gather(bf16[1,64,32]{1,2,0:T(8,128)(2,1)S(1)} %multiply_bitcast_fusion), channel_id=1, replica_groups=mesh['row'=4,'col'=8] {'col'}, dimensions={0}, use_global_device_ids=true | all-gather | bytes 36864 | tf_op jit(solution)/shard_map/all_gather | solution.py:107
  78.1 12.5 %all_gather.7 = bf16[32,512]{1,0:T(8,128)(2,1)S(1)} all-gather(bf16[32,128]{1,0:T(8,128)(2,1)S(1)} %multiply_convert_fusion.2), channel_id=1, replica_groups=mesh['row'=4,'col'=8] {'row'}, dimensions={1}, use_global_device_ids=true | all-gather | bytes 40960 | tf_op jit(solution)/shard_map/all_gather | solution.py:108
  92.4 5.2 %copy.105 = bf16[32,16,32,16]{0,1,3,2:T(8,128)(2,1)} copy(bf16[32,16,32,16]{2,3,1,0:T(8,128)(2,1)S(1)} %bitcast.246) | data formatting | bytes 1048576 | tf_op jit(solution)/shard_map/reshape | solution.py:20
  97.6 4.6 %reshape.55 = bf16[8,2,16384]{2,1,0:T(2,128)(2,1)} reshape(bf16[512,16,32]{2,1,0:T(8,128)(2,1)} %bitcast.247) | data formatting | bytes 1048576
  102.2 4.5 %all-to-all-start.2 = ((bf16[8,2,16384]{2,1,0:T(2,128)(2,1)}), bf16[8,2,16384]{2,1,0:T(2,128)(2,1)}, u32[]{:S(2)}, u32[]{:S(2)}) async-start(bf16[8,2,16384]{2,1,0:T(2,128)(2,1)} %reshape.55), calls=%async_computation.2 | async-start | bytes 1048576 | tf_op jit(solution)/shard_map/all_to_all | solution.py:25
  107.8 1.7 copy.97
  109.7 6.5 %all-to-all-done.2 = bf16[8,2,16384]{2,1,0:T(2,128)(2,1)} async-done(((bf16[8,2,16384]{2,1,0:T(2,128)(2,1)}), bf16[8,2,16384]{2,1,0:T(2,128)(2,1)}, u32[]{:S(2)}, u32[]{:S(2)}) %all-to-all-start.2) | async-done | bytes 524320 | tf_op jit(solution)/shard_map/all_to_all | solution.py:25
  116.3 3.1 %reshape.56 = bf16[512,16,32]{2,1,0:T(8,128)(2,1)S(1)} reshape(bf16[8,2,16384]{2,1,0:T(2,128)(2,1)} %all-to-all-done.2) | data formatting | bytes 1048576
  119.3 3.3 %copy.96 = bf16[32,8,16,64]{3,2,1,0:T(8,128)(2,1)} copy(bf16[32,8,16,64]{0,2,3,1:T(8,128)(2,1)S(1)} %bitcast.244) | data formatting | bytes 1048576 | tf_op jit(solution)/shard_map/all_to_all | solution.py:25
  122.6 2.9 %copy.98 = bf16[32,128,64]{2,0,1:T(8,128)(2,1)} copy(bf16[32,128,64]{2,1,0:T(8,128)(2,1)} %bitcast.250) | data formatting | bytes 1048576 | tf_op jit(solution)/shard_map/while | solution.py:97
  125.5 12.9 %while.40 = (s32[]{:T(128)}, bf16[32,128,64]{2,0,1:T(8,128)(2,1)}, bf16[32,128,64]{2,0,1:T(8,128)(2,1)}, bf16[32,128]{1,0:T(8,128)(2,1)S(1)}, bf16[32,128,64]{2,...) while((s32[]{:T(128)}, bf16[32,128,64]{2,0,1:T(8,128)(2,1)}, ...), condition=%wide.region_7.8_spmd, body=%wide.region_6.7_spmd.sunk | while | flops 119603200 | bytes 4334419 | solution.py:97
  127.5 1.3 fusion.150
  130.7 1.3 fusion.150
  133.9 1.3 fusion.150
  138.4 1.6 broadcast.30.clone
  140.0 13.3 %while.39 = (s32[]{:T(128)}, f32[32,128,64]{2,0,1:T(8,128)}, bf16[32,128,64]{2,0,1:T(8,128)(2,1)S(1)}, bf16[32,128]{1,0:T(8,128)(2,1)S(1)}, bf16[32,128,64]{2,0,...) while((s32[]{:T(128)}, f32[32,128,64]{2,0,1:T(8,128)}, ...), condition=%wide.region_5.6_spmd, body=%wide.region_4.5_spmd.sunk | while | flops 119603200 | bytes 4334419 | solution.py:97
  140.4 1.5 fusion.140
  142.0 1.4 fusion.141
  143.7 1.5 fusion.140
  145.3 1.4 fusion.141
  147.1 1.5 fusion.140
  148.6 1.4 fusion.141
  150.4 1.5 fusion.140
  152.0 1.4 fusion.141
  153.4 3.0 %fusion.98 = (f32[32,64]{1,0:T(8,128)S(1)}, f32[32,128]{0,1:T(8,128)S(1)}, bf16[32,128,64]{2,0,1:T(8,128)(2,1)S(1)}) fusion(f32[32,128,64]{2,0,1:T(8,128)} %get-tuple-element.803), kind=kLoop, calls=%fused_computation.128 | loop fusion | flops 780288 | bytes 1597440 | tf_op jit(solution)/shard_map/reduce_sum | solution.py:30
  156.3 18.0 %psum.31 = f32[32,64]{1,0:T(8,128)S(1)} all-reduce(f32[32,64]{1,0:T(8,128)S(1)} %get-tuple-element.773), channel_id=1, replica_groups=mesh['row'=4,'col'=8] {'row'}, use_global_device_ids=true, to_apply=%region_11.12 | all-reduce | flops 2048 | bytes 16384 | tf_op jit(solution)/shard_map/psum | solution.py:30
  174.4 22.3 %psum.30 = f32[32,128]{1,0:T(8,128)S(1)} all-reduce(f32[32,128]{1,0:T(8,128)S(1)} %copy.102), channel_id=1, replica_groups=mesh['row'=4,'col'=8] {'col'}, use_global_device_ids=true, to_apply=%region_9.10 | all-reduce | flops 4096 | bytes 32768 | tf_op jit(solution)/shard_map/psum | solution.py:29
  197.1 1.6 broadcast.30
  198.7 13.3 %while.41 = (s32[]{:T(128)}, f32[32,128,64]{2,0,1:T(8,128)}, bf16[32,128,64]{2,0,1:T(8,128)(2,1)S(1)}, bf16[32,128]{1,0:T(8,128)(2,1)S(1)}, bf16[32,128,64]{2,0,...) while((s32[]{:T(128)}, f32[32,128,64]{2,0,1:T(8,128)}, ...), condition=%wide.region_13.14_spmd, body=%wide.region_12.13_spmd.sunk | while | flops 119603200 | bytes 4334419 | solution.py:97
  199.1 1.5 fusion.158
  200.6 1.4 fusion.159
  202.4 1.5 fusion.158
  203.9 1.4 fusion.159
  205.7 1.5 fusion.158
  207.3 1.4 fusion.159
  209.1 1.5 fusion.158
  210.6 1.4 fusion.159
  212.0 3.6 %copy.103 = f32[32,128,64]{1,2,0:T(8,128)} copy(f32[32,128,64]{2,0,1:T(8,128)} %get-tuple-element.604) | data formatting | bytes 2097152 | tf_op jit(solution)/shard_map/while | solution.py:97
  (65 shorter events, 16.1 us)
Async XLA Ops:
  2.2 35.0 %copy-start.4 = (f32[2,128]{1,0:T(2,128)S(1)}, f32[2,128]{1,0:T(2,128)}, u32[]{:S(2)}) copy-start(f32[2,128]{1,0:T(2,128)} %param.15) | copy-start | bytes 3076
  2.2 35.0 %copy-start.5 = (f32[2,128]{1,0:T(2,128)S(1)}, f32[2,128]{1,0:T(2,128)}, u32[]{:S(2)}) copy-start(f32[2,128]{1,0:T(2,128)} %param.17) | copy-start | bytes 3076
  2.2 54.0 %copy-start.3 = (bf16[2,128,32]{1,2,0:T(8,128)(2,1)S(1)}, bf16[2,128,32]{1,2,0:T(8,128)(2,1)}, u32[]{:S(2)}) copy-start(bf16[2,128,32]{1,2,0:T(8,128)(2,1)} %param.18) | copy-start | bytes 49156
  5.4 50.9 %all-to-all-start = ((bf16[8,2,16384]{2,1,0:T(2,128)(2,1)}), bf16[8,2,16384]{2,1,0:T(2,128)(2,1)S(1)}, u32[]{:S(2)}, u32[]{:S(2)}) async-start(bf16[8,2,16384]{2,1,0:T(2,128)(2,1)} %reshape.53), calls=%async_computation | async-start | bytes 1048576 | tf_op jit(solution)/shard_map/all_to_all | solution.py:10
  63.9 4.4 %copy-start.6 = (f32[2,32]{1,0:T(2,128)S(1)}, f32[2,32]{1,0:T(2,128)}, u32[]{:S(2)}) copy-start(f32[2,32]{1,0:T(2,128)} %param.19) | copy-start | bytes 772
  64.0 26.7 %copy-start.1 = (bf16[2,128,128]{2,1,0:T(8,128)(2,1)S(1)}, bf16[2,128,128]{2,1,0:T(8,128)(2,1)}, u32[]{:S(2)}) copy-start(bf16[2,128,128]{2,1,0:T(8,128)(2,1)} %param.14) | copy-start | bytes 196612
  65.7 25.5 %all-to-all-start.1 = ((bf16[32,32,256]{2,0,1:T(8,128)(2,1)}), bf16[32,32,256]{2,0,1:T(8,128)(2,1)S(1)}, u32[]{:S(2)}, u32[]{:S(2)}) async-start(bf16[32,32,256]{2,0,1:T(8,128)(2,1)} %copy.91), calls=%async_computation.1 | async-start | bytes 1048576 | tf_op jit(solution)/shard_map/all_to_all | solution.py:18
  97.6 10.2 %copy-start = (f32[32,128,64]{1,2,0:T(8,128)S(1)}, f32[32,128,64]{1,2,0:T(8,128)}, u32[]{:S(2)}) copy-start(f32[32,128,64]{1,2,0:T(8,128)} %param.13) | copy-start | bytes 3145732
  102.2 7.4 %copy-start.2 = (bf16[2,128,128]{2,1,0:T(8,128)(2,1)S(1)}, bf16[2,128,128]{2,1,0:T(8,128)(2,1)}, u32[]{:S(2)}) copy-start(bf16[2,128,128]{2,1,0:T(8,128)(2,1)} %param.16) | copy-start | bytes 196612
  102.2 14.0 %all-to-all-start.2 = ((bf16[8,2,16384]{2,1,0:T(2,128)(2,1)}), bf16[8,2,16384]{2,1,0:T(2,128)(2,1)}, u32[]{:S(2)}, u32[]{:S(2)}) async-start(bf16[8,2,16384]{2,1,0:T(2,128)(2,1)} %reshape.55), calls=%async_computation.2 | async-start | bytes 1048576 | tf_op jit(solution)/shard_map/all_to_all | solution.py:25
where the time goes:
time: 217 us; the launch traced here: 216 us
  blocking collectives  108 us (50%)
  local copies, waits for them, and re-layouts  41.7 us (19%)
  matrix products  40.3 us (19%)
  starting transfers between devices  12.3 us (6%)
  waiting for transfers between devices  6.55 us (3%)
  other arithmetic  6.3 us (3%)
    psum x2, blocking collectives, pooled(): row_pool = lax.psum(jnp.sum(values, axis=2), 'col') * pool_scale  48.9 us
    psum x2, blocking collectives, pooled(): col_pool = lax.psum(jnp.sum(values, axis=1), 'row') * pool_scale  37 us
    dot_general x12, matrix products, fill_block(): jnp.einsum('kc,krj->crj', out_mat, second, preferred_element_type=jnp.flo...  16.5 us
    dot_general x12, matrix products, fill_block(): jnp.einsum('hk,hrj->krj', mid_mat, hidden, preferred_element_type=jnp.flo...  14.7 us
    all_gather x1, blocking collectives, body(): lax.all_gather(row_pool.astype(jnp.bfloat16), 'row', axis=1, tiled=True)  12.5 us
    unnamed x19, local copies, waits for them, and re-layouts  10 us
    all_gather x1, blocking collectives, body(): every_col = lax.all_gather(col_pool, 'col', axis=1, tiled=True)  9.59 us
    while x3, local copies, waits for them, and re-layouts, evaluate(): return lax.fori_loop(0, split_count, fill_block, result)  8.21 us
  transfers between devices with their start and end apart: 3, of which 1 were waited for; matrix products, arithmetic and copies ran while one was open for 2% of the time, Pallas kernels for 0%

commit v1 on v0

v1 whole, which is shorter than its diff:
```python
import functools
import math

import jax
import jax.numpy as jnp
from jax import lax
from jax.experimental import pallas as pl
from jax.experimental.pallas import tpu as pltpu
from jax.sharding import PartitionSpec as P

MESH = pl.DeviceIdType.MESH
BF = jnp.bfloat16
F32 = jnp.float32
LANES = 128


def dot(a, b):
    return jnp.dot(a, b, preferred_element_type=F32)


def kernel(
    dims,
    table,
    w_in,
    b_in,
    w_mid,
    b_mid,
    w_out,
    b_out,
    out,
    flat,
    turned,
    send,
    pair,
    own,
    own2,
    mir2,
    wt_in,
    wt_mid,
    bt_in,
    bt_mid,
    bt_out,
    spread,
    gather,
    col_chunks,
    row_part,
    col_part,
    row_recv,
    col_recv,
    mate_send,
    mate_recv,
    acc_row,
    acc_col,
    bulk_ssem,
    bulk_rsem,
    row_ssem,
    row_rsem,
    col_ssem,
    col_rsem,
    mate_ssem,
    mate_rsem,
):
    ch, tr, tc, n_row, n_col, q, nb, layers = dims
    pack = LANES // tc if tc < LANES else 1
    width = pack * tc
    bc = tc // nb
    lanes = bc * tr
    hid = w_mid.shape[1]
    scale = 1.0 / math.sqrt(tr * n_row)
    r = lax.axis_index("row")
    c = lax.axis_index("col")
    mir_r = c // q
    mir_c0 = q * r
    slot = c % q
    diag = mir_r == r

    barrier = pltpu.get_barrier_semaphore()
    for d in range(1, n_col):
        pl.semaphore_signal(
            barrier, inc=1, device_id=(r, lax.rem(c + d, n_col)), device_id_type=MESH
        )
    for d in range(1, n_row):
        pl.semaphore_signal(
            barrier, inc=1, device_id=(lax.rem(r + d, n_row), c), device_id_type=MESH
        )

    @pl.when(jnp.logical_not(diag))
    def _():
        for h in range(q):
            pl.semaphore_signal(
                barrier, inc=1, device_id=(mir_r, mir_c0 + h), device_id_type=MESH
            )

    groups = tr // LANES

    if groups > 1:
        for v in range(groups):
            flat[v * ch * tc : (v + 1) * ch * tc, :] = table[:, v * LANES : (v + 1) * LANES]

    def column_of(j):
        if groups == 1:
            return table[pl.ds(j, ch, stride=tc), :]
        parts = [flat[pl.ds(v * ch * tc + j, ch, stride=tc), :] for v in range(groups)]
        return jnp.concatenate(parts, axis=1)

    def turn_step(i, carry):
        src = pl.multiple_of(i * tc, tc)
        dst = pl.multiple_of(i * tr, tr)
        turned[pl.ds(dst, tr), :] = table[pl.ds(src, tc), :].T
        return carry

    lax.fori_loop(0, ch, turn_step, 0, unroll=4)

    def own_step(g, acc):
        for m in range(bc):
            val = column_of(g * bc + m)
            acc = acc + val
            own[g, :, m * tr : (m + 1) * tr] = val.astype(BF)
        return acc

    row_part[0] = lax.fori_loop(0, nb, own_step, jnp.zeros((ch, tr), F32))

    def col_step(i, acc):
        for u in range(8):
            acc = acc + turned[pl.ds(i * 8 + u, ch, stride=tr), :]
        return acc

    acc = lax.fori_loop(0, tr // 8, col_step, jnp.zeros((ch, tc), F32))
    col_part[0] = jnp.concatenate([acc] * pack, axis=1) if pack > 1 else acc

    @pl.when(diag)
    def _():
        pl.semaphore_wait(barrier, n_col - 1 + n_row - 1)

    @pl.when(jnp.logical_not(diag))
    def _():
        pl.semaphore_wait(barrier, n_col - 1 + n_row - 1 + q)

    def row_copy(layer, d):
        return pltpu.make_async_remote_copy(
            src_ref=row_part.at[layer],
            dst_ref=row_recv.at[layer, d - 1],
            send_sem=row_ssem.at[layer, d - 1],
            recv_sem=row_rsem.at[layer, d - 1],
            device_id=(r, lax.rem(c + d, n_col)),
            device_id_type=MESH,
        )

    def col_copy(layer, d):
        return pltpu.make_async_remote_copy(
            src_ref=col_part.at[layer],
            dst_ref=col_recv.at[layer, d - 1],
            send_sem=col_ssem.at[layer, d - 1],
            recv_sem=col_rsem.at[layer, d - 1],
            device_id=(lax.rem(r + d, n_row), c),
            device_id_type=MESH,
        )

    def pools_start(layer):
        for d in range(1, n_row):
            col_copy(layer, d).start()
        for d in range(1, n_col):
            row_copy(layer, d).start()

    def pools_finish(layer):
        row_sum = row_part[layer]
        col_sum = col_part[layer]
        for d in range(1, n_row):
            col_copy(layer, d).wait()
            col_sum = col_sum + col_recv[layer, d - 1]
        for d in range(1, n_col):
            row_copy(layer, d).wait()
            row_sum = row_sum + row_recv[layer, d - 1]
        return row_sum * scale, col_sum * scale

    pools_start(0)

    def bulk_copy(h, k):
        return pltpu.make_async_remote_copy(
            src_ref=send.at[h, k],
            dst_ref=pair.at[slot * nb + k],
            send_sem=bulk_ssem.at[h, k],
            recv_sem=bulk_rsem.at[slot * nb + k],
            device_id=(mir_r, mir_c0 + h),
            device_id_type=MESH,
        )

    def stay_copy(h, k):
        return pltpu.make_async_copy(
            send.at[h, k], pair.at[slot * nb + k], bulk_rsem.at[slot * nb + k]
        )

    for k in range(nb):
        for h in range(q):
            for m in range(bc // pack):
                base = h * tc + k * bc + m * pack
                parts = [turned[pl.ds(base + u, ch, stride=tr), :] for u in range(pack)]
                val = jnp.concatenate(parts, axis=1) if pack > 1 else parts[0]
                send[h, k, :, m * width : (m + 1) * width] = val.astype(BF)
        for h in range(q):
            here = jnp.logical_and(diag, slot == h)

            @pl.when(here)
            def _():
                stay_copy(h, k).start()

            @pl.when(jnp.logical_not(here))
            def _():
                bulk_copy(h, k).start()

    for layer in range(layers):
        wt_in[layer] = w_in[layer].astype(F32).T.astype(BF)
        wt_mid[layer] = w_mid[layer].astype(F32).T.astype(BF)
        bt_in[layer] = jnp.broadcast_to(b_in[layer : layer + 1, :], (LANES, hid)).T
        bt_mid[layer] = jnp.broadcast_to(b_mid[layer : layer + 1, :], (LANES, hid)).T
        bt_out[layer] = jnp.broadcast_to(b_out[layer : layer + 1, :], (LANES, ch)).T
    cell_col = lax.broadcasted_iota(jnp.int32, (bc, lanes), 1) // tr
    spread[...] = jnp.where(
        cell_col == lax.broadcasted_iota(jnp.int32, (bc, lanes), 0), 1.0, 0.0
    ).astype(BF)
    cell_col = lax.broadcasted_iota(jnp.int32, (lanes, width), 0) // tr
    gather[...] = jnp.where(
        cell_col == lax.broadcasted_iota(jnp.int32, (lanes, width), 1), 1.0, 0.0
    ).astype(BF)

    rp, cp = pools_finish(0)
    rp = rp.astype(BF)
    cp = cp.astype(BF)
    for h in range(q):
        half = rp[:, h * tc : (h + 1) * tc]
        half = jnp.concatenate([half] * pack, axis=1) if pack > 1 else half
        mate_send[h, :ch, :] = half
        mate_send[h, ch:, :] = cp

    def mate_copy(h):
        return pltpu.make_async_remote_copy(
            src_ref=mate_send.at[h],
            dst_ref=mate_recv.at[slot],
            send_sem=mate_ssem.at[h],
            recv_sem=mate_rsem.at[slot],
            device_id=(mir_r, mir_c0 + h),
            device_id_type=MESH,
        )

    def mate_stay(h):
        return pltpu.make_async_copy(mate_send.at[h], mate_recv.at[slot], mate_rsem.at[slot])

    for h in range(q):
        here = jnp.logical_and(diag, slot == h)

        @pl.when(here)
        def _():
            mate_stay(h).start()

        @pl.when(jnp.logical_not(here))
        def _():
            mate_copy(h).start()

    for t in range(q):
        pltpu.make_async_copy(mate_send.at[0], mate_recv.at[t], mate_rsem.at[t]).wait()
    cp_rows = jnp.concatenate([mate_recv[t, ch:, :tc] for t in range(q)], axis=1)
    rp_rows = rp
    for g in range(nb):
        col_chunks[g, :ch, :] = cp[:, g * bc : (g + 1) * bc]
        col_chunks[g, ch:, :] = mate_recv[0, :ch, g * bc : (g + 1) * bc]

    def tile(x):
        return jnp.concatenate([x] * (lanes // x.shape[1]), axis=1)

    def network(layer, feats):
        h1 = dot(wt_in[layer], feats) + tile(bt_in[layer])
        h1 = jnp.maximum(h1, 0.0).astype(BF)
        h2 = dot(wt_mid[layer], h1) + tile(bt_mid[layer])
        h2 = jnp.maximum(h2, 0.0).astype(BF)
        return dot(w_out[layer], h2) + tile(bt_out[layer])

    acc_row[...] = jnp.zeros_like(acc_row)
    acc_col[...] = jnp.zeros_like(acc_col)

    def layer_one(g, carry):
        for t in range(q):
            pltpu.make_async_copy(
                send.at[0, 0], pair.at[t * nb + g], bulk_rsem.at[t * nb + g]
            ).wait()
        mine = own[g]
        pieces = [
            pair[t * nb + g, :, a * tc : (a + 1) * tc] for a in range(bc) for t in range(q)
        ]
        theirs = jnp.concatenate(pieces, axis=1)
        wide = dot(col_chunks[g], spread[...]).astype(BF)
        straight = jnp.concatenate([mine, theirs, tile(rp_rows), wide[:ch]], axis=0)
        value = network(0, straight)
        top = value.astype(BF)
        own2[g] = top
        low = (value - top.astype(F32)).astype(BF)
        sums = dot(jnp.concatenate([top, low], axis=0), gather[...])
        sums = sums[:ch] + sums[ch:]
        acc_col[...] += pltpu.roll(sums, g * bc, 1)
        total = acc_row[...]
        for m in range(bc):
            total = total + value[:, m * tr : (m + 1) * tr]
        acc_row[...] = total
        mirrored = jnp.concatenate([theirs, mine, wide[ch:], tile(cp_rows)], axis=0)
        mir2[g] = network(0, mirrored).astype(BF)
        return carry

    lax.fori_loop(0, nb, layer_one, 0)
    row_part[1] = acc_row[...]
    col_part[1] = acc_col[...]
    pools_start(1)

    for k in range(nb):
        for h in range(q):
            here = jnp.logical_and(diag, slot == h)

            @pl.when(jnp.logical_not(here))
            def _():
                bulk_copy(h, k).wait_send()

    for h in range(q):
        here = jnp.logical_and(diag, slot == h)

        @pl.when(jnp.logical_not(here))
        def _():
            mate_copy(h).wait_send()

    rp, cp = pools_finish(1)
    rp_two = rp.astype(BF)
    cp = cp.astype(BF)
    for g in range(nb):
        col_chunks[g, :ch, :] = cp[:, g * bc : (g + 1) * bc]

    def layer_two(g, carry):
        wide = dot(col_chunks[g, :ch, :], spread[...]).astype(BF)
        feats = jnp.concatenate([own2[g], mir2[g], tile(rp_two), wide], axis=0)
        value = network(1, feats)
        for m in range(bc):
            for v in range(groups):
                at = m * tr + v * LANES
                rows = pl.ds(v * ch * tc + g * bc + m, ch, stride=tc)
                if groups == 1:
                    out[rows, :] = value[:, at : at + LANES]
                else:
                    flat[rows, :] = value[:, at : at + LANES]
        return carry

    lax.fori_loop(0, nb, layer_two, 0)
    if groups > 1:
        for v in range(groups):
            out[:, v * LANES : (v + 1) * LANES] = flat[v * ch * tc : (v + 1) * ch * tc, :]


def body(table, in_weight, in_bias, mid_weight, mid_bias, out_weight, out_bias):
    ch, tr, tc = table.shape
    n_row = lax.axis_size("row")
    n_col = lax.axis_size("col")
    layers, _, hid = in_weight.shape
    q = tr // tc
    assert tr == q * tc and n_col == q * n_row
    nb = 8
    pack = LANES // tc if tc < LANES else 1
    width = pack * tc
    bc = tc // nb
    lanes = bc * tr
    dims = (ch, tr, tc, n_row, n_col, q, nb, layers)
    dma = pltpu.SemaphoreType.DMA
    vmem = pl.BlockSpec(memory_space=pltpu.VMEM)
    result = pl.pallas_call(
        functools.partial(kernel, dims),
        out_shape=jax.ShapeDtypeStruct((ch * tc, tr), F32),
        in_specs=[vmem] * 7,
        out_specs=vmem,
        scratch_shapes=[
            pltpu.VMEM((tr // LANES * ch * tc if tr > LANES else 8, LANES), F32),
            pltpu.VMEM((ch * tr, tc), F32),
            pltpu.VMEM((q, nb, ch, bc * tc), BF),
            pltpu.VMEM((q * nb, ch, bc * tc), BF),
            pltpu.VMEM((nb, ch, lanes), BF),
            pltpu.VMEM((nb, ch, lanes), BF),
            pltpu.VMEM((nb, ch, lanes), BF),
            pltpu.VMEM((layers, hid, in_weight.shape[1]), BF),
            pltpu.VMEM((layers, hid, hid), BF),
            pltpu.VMEM((layers, hid, LANES), F32),
            pltpu.VMEM((layers, hid, LANES), F32),
            pltpu.VMEM((layers, ch, LANES), F32),
            pltpu.VMEM((bc, lanes), BF),
            pltpu.VMEM((lanes, width), BF),
            pltpu.VMEM((nb, 2 * ch, bc), BF),
            pltpu.VMEM((layers, ch, tr), F32),
            pltpu.VMEM((layers, ch, width), F32),
            pltpu.VMEM((layers, n_col - 1, ch, tr), F32),
            pltpu.VMEM((layers, n_row - 1, ch, width), F32),
            pltpu.VMEM((q, 2 * ch, width), BF),
            pltpu.VMEM((q, 2 * ch, width), BF),
            pltpu.VMEM((ch, tr), F32),
            pltpu.VMEM((ch, width), F32),
            dma((q, nb)),
            dma((q * nb,)),
            dma((layers, n_col - 1)),
            dma((layers, n_col - 1)),
            dma((layers, n_row - 1)),
            dma((layers, n_row - 1)),
            dma((q,)),
            dma((q,)),
        ],
        compiler_params=pltpu.CompilerParams(
            collective_id=0, has_side_effects=True, vmem_limit_bytes=60 * 1024 * 1024
        ),
    )(
        jnp.swapaxes(table, 1, 2).reshape(ch * tc, tr),
        in_weight,
        in_bias,
        mid_weight,
        mid_bias,
        jnp.swapaxes(out_weight, 1, 2),
        out_bias,
    )
    return jnp.swapaxes(result.reshape(ch, tc, tr), 1, 2)


def solution(mesh):
    placed = (P(None, "row", "col"), P(), P(), P(), P(), P(), P())
    return jax.shard_map(
        body, mesh=mesh, in_specs=placed, out_specs=P(None, "row", "col"), check_vma=False
    )
```

time: 217 us -> 68.3 us (0.31)
  blocking collectives: 108 us -> 0 us
  Pallas kernels: 0 us -> 65.9 us
  matrix products: 40.3 us -> 0 us
  local copies, waits for them, and re-layouts: 41.7 us -> 2.31 us
  starting transfers between devices: 12.3 us -> 0 us
  waiting for transfers between devices: 6.55 us -> 0 us
  other arithmetic: 6.3 us -> 0 us
    psum x4 -> x0, blocking collectives: 86 us -> none  [the longest x2 48.9 us: pooled(): row_pool = lax.psum(jnp.sum(values, axis=2), 'col') * pool_scale]
    pallas_call x0 -> x1, Pallas kernels: none -> 65.9 us  [body(): pl.pallas_call(functools.partial(kernel, dims), out_shape=jax.ShapeDtypeS...]
    dot_general x42 -> x0, matrix products: 40.3 us -> none  [the longest x12 16.5 us: fill_block(): jnp.einsum('kc,krj->crj', out_mat, second, preferred_element_type=jnp.flo...]
    all_gather x2 -> x0, blocking collectives: 22.1 us -> none  [the longest x1 12.5 us: body(): lax.all_gather(row_pool.astype(jnp.bfloat16), 'row', axis=1, tiled=True)]
    all_to_all x3 -> x0, starting transfers between devices: 12.3 us -> none  [the longest x1 5.2 us: to_strips(): lax.all_to_all(tile_in, 'col', split_axis=1, concat_axis=2, tiled=True)]
    while x3 -> x0, local copies, waits for them, and re-layouts: 8.21 us -> none  [evaluate(): return lax.fori_loop(0, split_count, fill_block, result)]
    unnamed x19 -> x1, local copies, waits for them, and re-layouts: 10 us -> 2.31 us
    reshape x2 -> x0, local copies, waits for them, and re-layouts: 6.99 us -> none  [the longest x1 5.23 us: swap_strips(): return regrouped.reshape(channels, piece_rows, entities)]
  transfers between devices with their start and end apart: 3 -> 0, of which waited for: 1 -> 0; matrix products, arithmetic and copies ran while one was open for 2% -> 0% of each run, Pallas kernels for 0% -> 0%
where the time goes in v1:
time: 68.3 us; the launch traced here: 68.2 us
  Pallas kernels  65.9 us (96%)
  local copies, waits for them, and re-layouts  2.31 us (3%)
    pallas_call x1, Pallas kernels, body(): pl.pallas_call(functools.partial(kernel, dims), out_shape=jax.ShapeDtypeS...  65.9 us
    unnamed x1, local copies, waits for them, and re-layouts  2.31 us

profile of v1, /device:TPU:0, one launch (start us, length us, event | category | flops | bytes accessed | tf_op | source)
XLA Modules:
  0.0 68.2 jit_solution(2568222829041841988)
XLA Ops:
  0.0 65.9 %shard_map.73 = f32[2048,128]{1,0:T(8,128)} custom-call(f32[2048,128]{1,0:T(8,128)} %bitcast.8, bf16[2,128,128]{2,1,0:T(8,128)(2,1)} %w_in.1, f32[2,128]{1,0:T(2,128)} %b_in.1, bf16[2,128,128]{2,1,0:T(8,128)(2,1)} %w_mid.1, f32[2,128]{1,0:T(2,128)} %b_mid.1, bf16[2,32,128]{2,1,0:T(8,128)(2,1)} %bitcast.9, f32[2,32]{1,0:T(2,128)} %b_out.1), custom_call_target="tpu_custom_call" | custom-call | tf_op jit(solution)/shard_map/pallas_call | solution.py:368
  65.9 2.3 %copy.9 = f32[32,128,64]{1,2,0:T(8,128)} copy(f32[32,128,64]{1,2,0:T(8,128)} %bitcast.7) | data formatting | bytes 2097152

commit v2 on v1

--- a/solution.py
+++ b/solution.py
@@ -32,6 +32,7 @@
     turned,
     send,
     pair,
+    relay,
     own,
     own2,
     mir2,
@@ -53,6 +54,8 @@
     acc_col,
     bulk_ssem,
     bulk_rsem,
+    relay_ssem,
+    relay_rsem,
     row_ssem,
     row_rsem,
     col_ssem,
@@ -185,6 +188,33 @@
             device_id_type=MESH,
         )
 
+    def first_leg(h, k):
+        d = lax.rem(mir_c0 + h - c + n_col, n_col)
+        return pltpu.make_async_remote_copy(
+            src_ref=send.at[h, k],
+            dst_ref=relay.at[d - 1, k // 2],
+            send_sem=bulk_ssem.at[h, k],
+            recv_sem=relay_rsem.at[d - 1, k // 2],
+            device_id=(r, mir_c0 + h),
+            device_id_type=MESH,
+        )
+
+    def second_leg(d, m):
+        start = lax.rem(c - d + n_col, n_col)
+        at = lax.rem(start, q) * nb + 2 * m + 1
+        return pltpu.make_async_remote_copy(
+            src_ref=relay.at[d - 1, m],
+            dst_ref=pair.at[at],
+            send_sem=relay_ssem.at[d - 1, m],
+            recv_sem=bulk_rsem.at[at],
+            device_id=(start // q, c),
+            device_id_type=MESH,
+        )
+
+    def relays(d):
+        start = lax.rem(c - d + n_col, n_col)
+        return jnp.logical_and(diag, start // q != r)
+
     def stay_copy(h, k):
         return pltpu.make_async_copy(
             send.at[h, k], pair.at[slot * nb + k], bulk_rsem.at[slot * nb + k]
@@ -204,9 +234,17 @@
             def _():
                 stay_copy(h, k).start()
 
-            @pl.when(jnp.logical_not(here))
+            direct = jnp.logical_not(here) if k % 2 == 0 else jnp.logical_and(diag, slot != h)
+
+            @pl.when(direct)
             def _():
                 bulk_copy(h, k).start()
+
+            if k % 2 == 1:
+
+                @pl.when(jnp.logical_not(diag))
+                def _():
+                    first_leg(h, k).start()
 
     for layer in range(layers):
         wt_in[layer] = w_in[layer].astype(F32).T.astype(BF)
@@ -278,6 +316,15 @@
     acc_col[...] = jnp.zeros_like(acc_col)
 
     def layer_one(g, carry):
+        for d in range(1, n_col):
+
+            @pl.when(jnp.logical_and(relays(d), g % 2 == 0))
+            def _():
+                pltpu.make_async_copy(
+                    send.at[0, 0], relay.at[d - 1, g // 2], relay_rsem.at[d - 1, g // 2]
+                ).wait()
+                second_leg(d, g // 2).start()
+
         for t in range(q):
             pltpu.make_async_copy(
                 send.at[0, 0], pair.at[t * nb + g], bulk_rsem.at[t * nb + g]
@@ -317,6 +364,13 @@
             def _():
                 bulk_copy(h, k).wait_send()
 
+    for d in range(1, n_col):
+
+        @pl.when(relays(d))
+        def _():
+            for m in range(nb // 2):
+                second_leg(d, m).wait_send()
+
     for h in range(q):
         here = jnp.logical_and(diag, slot == h)
 
@@ -375,6 +429,7 @@
             pltpu.VMEM((ch * tr, tc), F32),
             pltpu.VMEM((q, nb, ch, bc * tc), BF),
             pltpu.VMEM((q * nb, ch, bc * tc), BF),
+            pltpu.VMEM((n_col - 1, nb // 2, ch, bc * tc), BF),
             pltpu.VMEM((nb, ch, lanes), BF),
             pltpu.VMEM((nb, ch, lanes), BF),
             pltpu.VMEM((nb, ch, lanes), BF),
@@ -396,6 +451,8 @@
             pltpu.VMEM((ch, width), F32),
             dma((q, nb)),
             dma((q * nb,)),
+            dma((n_col - 1, nb // 2)),
+            dma((n_col - 1, nb // 2)),
             dma((layers, n_col - 1)),
             dma((layers, n_col - 1)),
             dma((layers, n_row - 1)),

time: 68.3 us -> 52.9 us (0.77)
  Pallas kernels: 65.9 us -> 50.4 us
    pallas_call x1, Pallas kernels: 65.9 us -> 50.4 us  [body(): pl.pallas_call(functools.partial(kernel, dims), out_shape=jax.ShapeDtypeS...]
where the time goes in v2:
time: 52.9 us; the launch traced here: 52.7 us
  Pallas kernels  50.4 us (95%)
  local copies, waits for them, and re-layouts  2.31 us (4%)
    pallas_call x1, Pallas kernels, body(): pl.pallas_call(functools.partial(kernel, dims), out_shape=jax.ShapeDtypeS...  50.4 us
    unnamed x1, local copies, waits for them, and re-layouts  2.31 us

profile of v2, /device:TPU:0, one launch (start us, length us, event | category | flops | bytes accessed | tf_op | source)
XLA Modules:
  0.0 52.7 jit_solution(4814402756132990215)
XLA Ops:
  0.0 50.4 %shard_map.73 = f32[2048,128]{1,0:T(8,128)} custom-call(f32[2048,128]{1,0:T(8,128)} %bitcast.8, bf16[2,128,128]{2,1,0:T(8,128)(2,1)} %w_in.1, f32[2,128]{1,0:T(2,128)} %b_in.1, bf16[2,128,128]{2,1,0:T(8,128)(2,1)} %w_mid.1, f32[2,128]{1,0:T(2,128)} %b_mid.1, bf16[2,32,128]{2,1,0:T(8,128)(2,1)} %bitcast.9, f32[2,32]{1,0:T(2,128)} %b_out.1), custom_call_target="tpu_custom_call" | custom-call | tf_op jit(solution)/shard_map/pallas_call | solution.py:422
  50.4 2.3 %copy.9 = f32[32,128,64]{1,2,0:T(8,128)} copy(f32[32,128,64]{1,2,0:T(8,128)} %bitcast.7) | data formatting | bytes 2097152

commit v3 on v2

--- a/solution.py
+++ b/solution.py
@@ -315,6 +315,14 @@
     acc_row[...] = jnp.zeros_like(acc_row)
     acc_col[...] = jnp.zeros_like(acc_col)
 
+    late = nb // 2 - 1
+
+    def mirror_one(g, carry):
+        wide = dot(col_chunks[g, ch:, :], spread[...]).astype(BF)
+        mirrored = jnp.concatenate([mir2[g], own[g], wide, tile(cp_rows)], axis=0)
+        mir2[g] = network(0, mirrored).astype(BF)
+        return carry
+
     def layer_one(g, carry):
         for d in range(1, n_col):
 
@@ -334,8 +342,9 @@
             pair[t * nb + g, :, a * tc : (a + 1) * tc] for a in range(bc) for t in range(q)
         ]
         theirs = jnp.concatenate(pieces, axis=1)
-        wide = dot(col_chunks[g], spread[...]).astype(BF)
-        straight = jnp.concatenate([mine, theirs, tile(rp_rows), wide[:ch]], axis=0)
+        mir2[g] = theirs
+        wide = dot(col_chunks[g, :ch, :], spread[...]).astype(BF)
+        straight = jnp.concatenate([mine, theirs, tile(rp_rows), wide], axis=0)
         value = network(0, straight)
         top = value.astype(BF)
         own2[g] = top
@@ -347,14 +356,19 @@
         for m in range(bc):
             total = total + value[:, m * tr : (m + 1) * tr]
         acc_row[...] = total
-        mirrored = jnp.concatenate([theirs, mine, wide[ch:], tile(cp_rows)], axis=0)
-        mir2[g] = network(0, mirrored).astype(BF)
+
+        @pl.when(g < nb - late)
+        def _():
+            mirror_one(g, 0)
+
         return carry
 
     lax.fori_loop(0, nb, layer_one, 0)
     row_part[1] = acc_row[...]
     col_part[1] = acc_col[...]
     pools_start(1)
+
+    lax.fori_loop(nb - late, nb, mirror_one, 0)
 
     for k in range(nb):
         for h in range(q):

time: 52.9 us -> 52.6 us (level)
  no operation moved by 1% of the time
where the time goes in v3:
time: 52.6 us; the launch traced here: 52.4 us
  Pallas kernels  50.1 us (95%)
  local copies, waits for them, and re-layouts  2.31 us (4%)
    pallas_call x1, Pallas kernels, body(): pl.pallas_call(functools.partial(kernel, dims), out_shape=jax.ShapeDtypeS...  50.1 us
    unnamed x1, local copies, waits for them, and re-layouts  2.31 us

profile of v3, /device:TPU:0, one launch (start us, length us, event | category | flops | bytes accessed | tf_op | source)
XLA Modules:
  0.0 52.4 jit_solution(9751455458915507194)
XLA Ops:
  0.0 50.1 %shard_map.73 = f32[2048,128]{1,0:T(8,128)} custom-call(f32[2048,128]{1,0:T(8,128)} %bitcast.8, bf16[2,128,128]{2,1,0:T(8,128)(2,1)} %w_in.1, f32[2,128]{1,0:T(2,128)} %b_in.1, bf16[2,128,128]{2,1,0:T(8,128)(2,1)} %w_mid.1, f32[2,128]{1,0:T(2,128)} %b_mid.1, bf16[2,32,128]{2,1,0:T(8,128)(2,1)} %bitcast.9, f32[2,32]{1,0:T(2,128)} %b_out.1), custom_call_target="tpu_custom_call" | custom-call | tf_op jit(solution)/shard_map/pallas_call | solution.py:436
  50.1 2.3 %copy.9 = f32[32,128,64]{1,2,0:T(8,128)} copy(f32[32,128,64]{1,2,0:T(8,128)} %bitcast.7) | data formatting | bytes 2097152
